TPU v7x, 32 devices: a whole 2x2x4 slice. The times are simulated.
32 devices in a mesh: groups: 2 (over x), gy: 16 (over z, y, core).
Axes of the slice: x: 2, y: 2, z: 4, core: 2. Of those that a mesh axis runs over, the one named last changes fastest.
Arguments:
- observed: float32 [2048, 16, 256], P(('groups', 'gy')), parts along dimension 0, may hold values from -6 to 6
- tf_table: float32 [16], replicated, may hold values from 0.2 to 2
- tilt_index: int32 [513, 129], replicated, may hold values from 0 to 15
- wedge: int32 [513, 129], replicated, may hold values 0 or 1
Outputs:
- restored: float32 [2048, 16, 256], P(('groups', 'gy')), parts along dimension 0
There are 2 independent parts, one for each index of `groups`. A program takes and returns all parts, laid end to end along the dimension named above; an argument that names none is the same for every part. Nothing has to cross between parts.
All inputs are finite; a program needn't handle non-finite values.
Results may differ from a plain program's by a relative error of at most 0.00011.
Values sent between devices are 32-bit elements; how exact they have to be, the bound alone decides.
A program may use at most 64 MiB of HBM per device.

v0:
```python
import math

import jax
import jax.numpy as jnp
from jax import lax
from jax.sharding import PartitionSpec as P

NX = 1024
OUTER = 2
PASSES = 2


step_dual = 0.14
step_primal = 0.14
huber_eps = 0.05
bound_dual = 0.5
highest = lax.Precision.HIGHEST


def extended(value, sides, width):
    for axis, dim in sides:
        devices, length = (lax.axis_size(axis), value.shape[dim])
        up = [(i, (i + 1) % devices) for i in range(devices - 1)]
        down = [(j, i) for i, j in up]
        last = lax.slice_in_dim(value, length - width, length, axis=dim)
        initial = lax.slice_in_dim(value, 0, width, axis=dim)
        before = lax.ppermute(last, axis, up)
        after = lax.ppermute(initial, axis, down)
        value = jnp.concatenate([before, value, after], axis=dim)
    return value


def curvature(field, axis):
    widths = [(0, 0), (0, 0), (0, 0)]
    widths[axis] = (1, 1)
    padded = jnp.pad(field, widths)
    upper = lax.slice_in_dim(padded, 2, padded.shape[axis], axis=axis)
    lower = lax.slice_in_dim(padded, 0, padded.shape[axis] - 2, axis=axis)
    return upper + lower - 2.0 * field


def rim_curvature(padded, field, axis):
    upper = lax.slice_in_dim(padded, 2, padded.shape[axis], axis=axis)
    lower = lax.slice_in_dim(padded, 0, padded.shape[axis] - 2, axis=axis)
    return upper + lower - 2.0 * field


def denoise(target, duals, sharded, primal_rim, dual_rim):
    field = target
    lead = target
    for sweep in range(PASSES):
        padded = primal_rim(lead)
        raised = []
        for axis in range(3):
            if axis == sharded:
                bend = rim_curvature(padded, lead, axis)
            else:
                bend = curvature(lead, axis)
            raised.append(
                (duals[axis] + step_dual * bend) / (1.0 + step_dual * huber_eps / bound_dual)
            )
        total = raised[0] * raised[0] + raised[1] * raised[1] + raised[2] * raised[2]
        shrink = jnp.sqrt(jnp.maximum(1.0, total / (bound_dual * bound_dual)))
        duals = (raised[0] / shrink, raised[1] / shrink, raised[2] / shrink)
        padded_dual = dual_rim(duals[sharded])
        adjoint = jnp.zeros_like(field)
        for axis in range(3):
            if axis == sharded:
                adjoint = rim_curvature(padded_dual, duals[axis], axis)
            else:
                adjoint = adjoint + curvature(duals[axis], axis)
        updated = (field - step_primal * adjoint + step_primal * target) / (1.0 + step_primal)
        lead = 2.0 * updated - field
        field = updated
    return (field, duals)


def z_tables(length):
    half = length // 2
    position = jnp.arange(length, dtype=jnp.int32)
    column = jnp.arange(length, dtype=jnp.int32)
    is_cosine = column <= half
    frequency = jnp.where(is_cosine, column, column - half)
    phase = position[:, None] * frequency[None, :] % length
    angle = phase.astype(jnp.float32) * (2.0 * math.pi / length)
    forward = jnp.where(is_cosine[None, :], jnp.cos(angle), jnp.sin(angle))
    weight = jnp.where((column == 0) | (column == half), 1.0, 2.0) / length
    backward = forward.T * weight[:, None]
    return (forward, backward)


def x_tables(length):
    half = length // 2
    freqs = jnp.arange(half + 1, dtype=jnp.int32)
    position = jnp.arange(length, dtype=jnp.int32)
    phase = freqs[:, None] * position[None, :] % length
    angle = phase.astype(jnp.float32) * (2.0 * math.pi / length)
    cos_table = jnp.cos(angle)
    sin_table = jnp.sin(angle)
    weight = jnp.where((freqs == 0) | (freqs == half), 1.0, 2.0) / length
    return (cos_table, sin_table, (cos_table * weight[:, None]).T, (sin_table * weight[:, None]).T)


def x_forward(columns, cos_table, sin_table):
    flat = columns.reshape(columns.shape[0], -1)
    shape_out = (cos_table.shape[0],) + columns.shape[1:]
    real_part = jnp.dot(cos_table, flat, precision=highest).reshape(shape_out)
    imag_part = jnp.dot(sin_table, flat, precision=highest).reshape(shape_out)
    return (real_part, imag_part)


def x_inverse(real_part, imag_part, cos_back, sin_back):
    rows = real_part.shape[0]
    flat_real = real_part.reshape(rows, -1)
    flat_imag = imag_part.reshape(rows, -1)
    summed = jnp.dot(cos_back, flat_real, precision=highest) + jnp.dot(
        sin_back, flat_imag, precision=highest
    )
    return summed.reshape((cos_back.shape[0],) + real_part.shape[1:])


def filters(tf_table, tilt_index, wedge, length_z):
    levels = jnp.arange(tf_table.shape[0], dtype=jnp.int32)
    picked = jnp.sum(jnp.where(tilt_index[:, :, None] == levels, tf_table, 0.0), axis=2)
    half_rows = picked * wedge.astype(jnp.float32)
    response = jnp.concatenate([half_rows, half_rows[:, 1 : length_z // 2]], 1)
    denom = response * response + 1.0
    return ((response / denom)[:, None, :], (1.0 / denom)[:, None, :])


def rim_x_primal(field):
    return extended(field, (("gy", 0),), 1)


def rim_x_dual(field):
    return extended(field, (("gy", 0),), 1)


def local(observed, tf_table, tilt_index, wedge):
    length_z = observed.shape[2]
    forward_z, backward_z = z_tables(length_z)
    cos_table, sin_table, cos_back, sin_back = x_tables(NX)
    g_data, g_prior = filters(tf_table, tilt_index, wedge, length_z)
    packed = jnp.dot(observed, forward_z, precision=highest)
    columns = lax.all_to_all(packed, "gy", split_axis=1, concat_axis=0, tiled=True)
    data_real, data_imag = x_forward(columns, cos_table, sin_table)
    prior_real, prior_imag = (data_real, data_imag)
    current = observed
    duals = (jnp.zeros_like(observed), jnp.zeros_like(observed), jnp.zeros_like(observed))
    for outer in range(OUTER):
        if outer > 0:
            again = lax.all_to_all(
                jnp.dot(current, forward_z, precision=highest),
                "gy",
                split_axis=1,
                concat_axis=0,
                tiled=True,
            )
            prior_real, prior_imag = x_forward(again, cos_table, sin_table)
        merged = x_inverse(
            g_data * data_real + g_prior * prior_real,
            g_data * data_imag + g_prior * prior_imag,
            cos_back,
            sin_back,
        )
        slabs = lax.all_to_all(merged, "gy", split_axis=0, concat_axis=1, tiled=True)
        target = jnp.dot(slabs, backward_z, precision=highest)
        current, duals = denoise(target, duals, 0, rim_x_primal, rim_x_dual)
    return current


def solution(mesh):
    in_specs = (P(("groups", "gy"), None, None), P(), P(), P())
    out_specs = P(("groups", "gy"), None, None)
    return jax.shard_map(local, mesh=mesh, in_specs=in_specs, out_specs=out_specs, check_vma=False)
```

profile of v0, /device:TPU:16, one launch (start us, length us, event | category | flops | bytes accessed | tf_op | source)
XLA Modules:
  0.0 303.8 jit_solution(17991332169227890438)
XLA Ops:
  1.2 3.4 %convolution_bitcast_fusion = f32[64,16,256]{2,0,1:T(8,128)} fusion(f32[64,16,256]{2,1,0:T(8,128)S(1)} %copy-done, s32[256]{0:T(256)S(1)} %add_select_fusion.3, pred[256]{0:T(512)(128)(4,1)S(1)} %iota_compare_fusion.3), kind=kOutput, calls=%fused_computation.55 | convolution fusion | flops 806289408 | bytes 2098432 | tf_op jit(solution)/shard_map/dot_general | solution.py:144
  4.7 6.8 %all-to-all-start = ((f32[64,16,256]{2,0,1:T(8,128)}), f32[64,16,256]{2,0,1:T(8,128)S(1)}, u32[]{:S(2)}, u32[]{:S(2)}) async-start(f32[64,16,256]{2,0,1:T(8,128)} %convolution_bitcast_fusion), calls=%async_computation | async-start | bytes 2097152 | tf_op jit(solution)/shard_map/all_to_all | solution.py:145
  11.5 1.8 select_reduce_fusion
  13.4 22.8 %all-to-all-done = f32[64,16,256]{2,0,1:T(8,128)S(1)} async-done(((f32[64,16,256]{2,0,1:T(8,128)}), f32[64,16,256]{2,0,1:T(8,128)S(1)}, u32[]{:S(2)}, u32[]{:S(2)}) %all-to-all-start) | async-done | bytes 1048608 | tf_op jit(solution)/shard_map/all_to_all | solution.py:145
  36.1 10.8 %fusion.41 = f32[513,256]{0,1:T(8,128)S(1)} fusion(f32[1024,256]{1,0:T(8,128)S(1)} %bitcast.46), kind=kOutput, calls=%fused_computation.67 | convolution fusion | flops 1621112832 | bytes 1573888 | tf_op jit(solution)/shard_map/dot_general | solution.py:108
  46.9 10.5 %fusion.36 = f32[513,256]{0,1:T(8,128)S(1)} fusion(f32[1024,256]{1,0:T(8,128)S(1)} %bitcast.47), kind=kOutput, calls=%fused_computation.66 | convolution fusion | flops 1621112832 | bytes 1573888 | tf_op jit(solution)/shard_map/dot_general | solution.py:107
  57.4 12.6 %fusion.8 = f32[1024,256]{1,0:T(8,128)S(1)} fusion(f32[513]{0:T(1024)S(1)} %select_multiply_fusion.3, f32[513,256]{0,1:T(8,128)S(1)} %fusion.41, f32[513,127]{0,1:T(8,128)S(1)} %slice.276, f32[513,129]{0,1:T(8,128)S(1)} %convert_multiply_fusion), kind=kOutput, calls=%fused_computation.13 | convolution fusion | flops 1622688768 | bytes 2101252 | tf_op jit(solution)/shard_map/dot_general | solution.py:116
  70.1 12.1 %fusion.17 = f32[1024,1,256]{2,0,1:T(8,128)S(1)} fusion(f32[1024,256]{1,0:T(8,128)S(1)} %fusion.8, f32[513]{0:T(1024)S(1)} %select_multiply_fusion.3, f32[513,256]{0,1:T(8,128)S(1)} %fusion.36, f32[513,127]{0,1:T(8,128)S(1)} %slice.276, f32[513,129]{0,1:T(8,128)S(1)} %convert_multiply_fusion), kind=kOutput, calls=%fused_computation.52 | convolution fusion | flops 1622950912 | bytes 3149828 | tf_op jit(solution)/shard_map/dot_general | solution.py:116
  82.2 2.0 copy.43
  84.2 4.5 %all-to-all-start.1 = ((f32[1024,1,256]{2,1,0:T(1,128)}), f32[1024,1,256]{2,1,0:T(1,128)S(1)}, u32[]{:S(2)}, u32[]{:S(2)}) async-start(f32[1024,1,256]{2,1,0:T(1,128)} %copy.43), calls=%async_computation.1 | async-start | bytes 2097152 | tf_op jit(solution)/shard_map/all_to_all | solution.py:166
  88.8 25.1 %all-to-all-done.1 = f32[1024,1,256]{2,1,0:T(1,128)S(1)} async-done(((f32[1024,1,256]{2,1,0:T(1,128)}), f32[1024,1,256]{2,1,0:T(1,128)S(1)}, u32[]{:S(2)}, u32[]{:S(2)}) %all-to-all-start.1) | async-done | bytes 1048608 | tf_op jit(solution)/shard_map/all_to_all | solution.py:166
  114.0 2.6 fusion.146
  116.7 2.8 collective-permute-start
  119.5 1.9 collective-permute-start.1
  121.4 4.0 %collective-permute-done.1 = f32[1,16,256]{2,1,0:T(8,128)S(1)} collective-permute-done((f32[1,16,256]{2,1,0:T(8,128)S(1)}, f32[1,16,256]{2,1,0:T(8,128)S(1)}, u32[]{:S(2)}, u32[]{:S(2)}) %collective-permute-start.1) | collective-permute-done | bytes 16416 | tf_op jit(solution)/shard_map/ppermute | solution.py:27
  126.7 1.9 collective-permute-start.2
  128.6 2.4 collective-permute-start.3
  131.9 2.7 collective-permute-done.3
  135.6 1.9 collective-permute-start.4
  137.5 2.4 collective-permute-start.5
  139.9 3.5 %collective-permute-done.5 = f32[1,16,256]{2,1,0:T(8,128)S(1)} collective-permute-done((f32[1,16,256]{2,1,0:T(8,128)S(1)}, f32[1,16,256]{2,1,0:T(8,128)S(1)}, u32[]{:S(2)}, u32[]{:S(2)}) %collective-permute-start.5) | collective-permute-done | bytes 16416 | tf_op jit(solution)/shard_map/ppermute | solution.py:27
  143.4 1.6 fusion.238
  145.0 1.9 collective-permute-start.6
  146.9 2.4 collective-permute-start.7
  149.8 3.1 %collective-permute-done.7 = f32[1,16,256]{2,1,0:T(8,128)S(1)} collective-permute-done((f32[1,16,256]{2,1,0:T(8,128)S(1)}, f32[1,16,256]{2,1,0:T(8,128)S(1)}, u32[]{:S(2)}, u32[]{:S(2)}) %collective-permute-start.7) | collective-permute-done | bytes 16416 | tf_op jit(solution)/shard_map/ppermute | solution.py:27
  154.0 2.5 fusion.148
  156.5 29.2 %all_to_all.66 = f32[64,16,256]{2,0,1:T(8,128)S(1)} all-to-all(f32[64,16,256]{2,0,1:T(8,128)S(1)} %fusion.148), channel_id=1, replica_groups=mesh['groups'=2,'gy'=16] {'gy'}, dimensions={1} | all-to-all | bytes 2097152 | tf_op jit(solution)/shard_map/all_to_all | solution.py:152
  185.8 10.7 %fusion.26 = f32[513,256]{0,1:T(8,128)S(1)} fusion(f32[1024,256]{1,0:T(8,128)S(1)} %bitcast.48, f32[513,256]{0,1:T(8,128)S(1)} %copy-done.5, f32[513,127]{0,1:T(8,128)S(1)} %slice.276, f32[513,129]{0,1:T(8,128)S(1)} %convert_multiply_fusion), kind=kOutput, calls=%fused_computation.57 | convolution fusion | flops 1622163456 | bytes 2624512 | tf_op jit(solution)/shard_map/dot_general | solution.py:108
  196.4 10.7 %fusion.27 = f32[513,256]{0,1:T(8,128)S(1)} fusion(f32[1024,256]{1,0:T(8,128)S(1)} %bitcast.49, f32[513,256]{0,1:T(8,128)S(1)} %fusion.36, f32[513,127]{0,1:T(8,128)S(1)} %slice.276, f32[513,129]{0,1:T(8,128)S(1)} %convert_multiply_fusion), kind=kOutput, calls=%fused_computation.59 | convolution fusion | flops 1622163456 | bytes 2624512 | tf_op jit(solution)/shard_map/dot_general | solution.py:107
  207.2 12.1 %fusion.6 = f32[1024,256]{1,0:T(8,128)S(1)} fusion(f32[513,256]{0,1:T(8,128)S(1)} %fusion.26, f32[513]{0:T(1024)S(1)} %select_multiply_fusion.3), kind=kOutput, calls=%fused_computation.11 | convolution fusion | flops 1621638144 | bytes 1575940 | tf_op jit(solution)/shard_map/dot_general | solution.py:116
  219.3 12.3 %fusion.23 = f32[1024,1,256]{2,0,1:T(8,128)S(1)} fusion(f32[1024,256]{1,0:T(8,128)S(1)} %fusion.6, f32[513,256]{0,1:T(8,128)S(1)} %fusion.27, f32[513]{0:T(1024)S(1)} %select_multiply_fusion.3), kind=kOutput, calls=%fused_computation.54 | convolution fusion | flops 1621900288 | bytes 2624516 | tf_op jit(solution)/shard_map/dot_general | solution.py:116
  232.9 29.5 %all_to_all.67 = f32[1024,1,256]{2,1,0:T(1,128)S(1)} all-to-all(f32[1024,1,256]{2,1,0:T(1,128)S(1)} %copy.48), channel_id=1, replica_groups=mesh['groups'=2,'gy'=16] {'gy'}, dimensions={0} | all-to-all | bytes 2097152 | tf_op jit(solution)/shard_map/all_to_all | solution.py:166
  262.5 2.6 fusion.144
  265.1 2.8 collective-permute-start.8
  267.9 1.9 collective-permute-start.9
  269.9 4.0 %collective-permute-done.9 = f32[1,16,256]{2,1,0:T(8,128)S(1)} collective-permute-done((f32[1,16,256]{2,1,0:T(8,128)S(1)}, f32[1,16,256]{2,1,0:T(8,128)S(1)}, u32[]{:S(2)}, u32[]{:S(2)}) %collective-permute-start.9) | collective-permute-done | bytes 16416 | tf_op jit(solution)/shard_map/ppermute | solution.py:27
  273.9 1.6 fusion.239
  275.4 1.9 collective-permute-start.10
  277.4 2.4 collective-permute-start.11
  280.2 3.1 %collective-permute-done.11 = f32[1,16,256]{2,1,0:T(8,128)S(1)} collective-permute-done((f32[1,16,256]{2,1,0:T(8,128)S(1)}, f32[1,16,256]{2,1,0:T(8,128)S(1)}, u32[]{:S(2)}, u32[]{:S(2)}) %collective-permute-start.11) | collective-permute-done | bytes 16416 | tf_op jit(solution)/shard_map/ppermute | solution.py:27
  284.3 1.9 collective-permute-start.12
  286.2 2.4 collective-permute-start.13
  288.6 3.5 %collective-permute-done.13 = f32[1,16,256]{2,1,0:T(8,128)S(1)} collective-permute-done((f32[1,16,256]{2,1,0:T(8,128)S(1)}, f32[1,16,256]{2,1,0:T(8,128)S(1)}, u32[]{:S(2)}, u32[]{:S(2)}) %collective-permute-start.13) | collective-permute-done | bytes 16416 | tf_op jit(solution)/shard_map/ppermute | solution.py:27
  292.2 1.6 fusion.240
  293.7 1.9 collective-permute-start.14
  295.7 2.4 collective-permute-start.15
  298.5 3.1 %collective-permute-done.15 = f32[1,16,256]{2,1,0:T(8,128)S(1)} collective-permute-done((f32[1,16,256]{2,1,0:T(8,128)S(1)}, f32[1,16,256]{2,1,0:T(8,128)S(1)}, u32[]{:S(2)}, u32[]{:S(2)}) %collective-permute-start.15) | collective-permute-done | bytes 16416 | tf_op jit(solution)/shard_map/ppermute | solution.py:27
  301.6 2.0 fusion.115
  (45 shorter events, 9.1 us)
Async XLA Ops:
  0.0 1.2 copy-start
  4.7 6.8 %copy-start.1 = (s32[513,129]{0,1:T(8,128)S(1)}, s32[513,129]{0,1:T(8,128)}, u32[]{:S(2)}) copy-start(s32[513,129]{0,1:T(8,128)} %param.6) | copy-start | bytes 794128
  4.7 6.8 %copy-start.3 = (f32[16]{0:T(128)S(1)}, f32[16]{0:T(128)}, u32[]{:S(2)}) copy-start(f32[16]{0:T(128)} %param.5) | copy-start | bytes 196
  4.7 8.6 %copy-start.2 = (s32[513,129]{0,1:T(8,128)S(1)}, s32[513,129]{0,1:T(8,128)}, u32[]{:S(2)}) copy-start(s32[513,129]{0,1:T(8,128)} %param.7) | copy-start | bytes 794128
  4.7 31.5 %all-to-all-start = ((f32[64,16,256]{2,0,1:T(8,128)}), f32[64,16,256]{2,0,1:T(8,128)S(1)}, u32[]{:S(2)}, u32[]{:S(2)}) async-start(f32[64,16,256]{2,0,1:T(8,128)} %convolution_bitcast_fusion), calls=%async_computation | async-start | bytes 2097152 | tf_op jit(solution)/shard_map/all_to_all | solution.py:145
  46.9 10.5 %copy-start.4 = (f32[513,256]{0,1:T(8,128)}, f32[513,256]{0,1:T(8,128)S(1)}, u32[]{:S(2)}) copy-start(f32[513,256]{0,1:T(8,128)S(1)} %fusion.41) | copy-start | bytes 1575940
  84.2 29.7 %all-to-all-start.1 = ((f32[1024,1,256]{2,1,0:T(1,128)}), f32[1024,1,256]{2,1,0:T(1,128)S(1)}, u32[]{:S(2)}, u32[]{:S(2)}) async-start(f32[1024,1,256]{2,1,0:T(1,128)} %copy.43), calls=%async_computation.1 | async-start | bytes 2097152 | tf_op jit(solution)/shard_map/all_to_all | solution.py:166
  116.7 4.7 %collective-permute-start = (f32[1,16,256]{2,1,0:T(8,128)S(1)}, f32[1,16,256]{2,1,0:T(8,128)S(1)}, u32[]{:S(2)}, u32[]{:S(2)}) collective-permute-start(f32[1,16,256]{2,1,0:T(8,128)S(1)} %get-tuple-element.45), channel_id=1, source_target_pairs={{1,0},{2,1},{3,2},{4,3},{5,4},{6,5},{7,6},{8,7},{9,8},{10,9},{11,1... | collective-permute-start | bytes 49160 | tf_op jit(solution)/shard_map/ppermute | solution.py:28
  119.5 6.0 %collective-permute-start.1 = (f32[1,16,256]{2,1,0:T(8,128)S(1)}, f32[1,16,256]{2,1,0:T(8,128)S(1)}, u32[]{:S(2)}, u32[]{:S(2)}) collective-permute-start(f32[1,16,256]{2,1,0:T(8,128)S(1)} %get-tuple-element.46), channel_id=1, source_target_pairs={{0,1},{1,2},{2,3},{3,4},{4,5},{5,6},{6,7},{7,8},{8,9},{9,10},{10,1... | collective-permute-start | bytes 49160 | tf_op jit(solution)/shard_map/ppermute | solution.py:27
  126.7 5.1 %collective-permute-start.2 = (f32[1,16,256]{2,1,0:T(8,128)S(1)}, f32[1,16,256]{2,1,0:T(8,128)S(1)}, u32[]{:S(2)}, u32[]{:S(2)}) collective-permute-start(f32[1,16,256]{2,1,0:T(8,128)S(1)} %get-tuple-element.43), channel_id=1, source_target_pairs={{1,0},{2,1},{3,2},{4,3},{5,4},{6,5},{7,6},{8,7},{9,8},{10,9},{11,1... | collective-permute-start | bytes 49160 | tf_op jit(solution)/shard_map/ppermute | solution.py:28
  128.6 6.0 %collective-permute-start.3 = (f32[1,16,256]{2,1,0:T(8,128)S(1)}, f32[1,16,256]{2,1,0:T(8,128)S(1)}, u32[]{:S(2)}, u32[]{:S(2)}) collective-permute-start(f32[1,16,256]{2,1,0:T(8,128)S(1)} %get-tuple-element.44), channel_id=1, source_target_pairs={{0,1},{1,2},{2,3},{3,4},{4,5},{5,6},{6,7},{7,8},{8,9},{9,10},{10,1... | collective-permute-start | bytes 49160 | tf_op jit(solution)/shard_map/ppermute | solution.py:27
  135.6 4.3 %collective-permute-start.4 = (f32[1,16,256]{2,1,0:T(8,128)S(1)}, f32[1,16,256]{2,1,0:T(8,128)S(1)}, u32[]{:S(2)}, u32[]{:S(2)}) collective-permute-start(f32[1,16,256]{2,1,0:T(8,128)S(1)} %get-tuple-element.41), channel_id=1, source_target_pairs={{1,0},{2,1},{3,2},{4,3},{5,4},{6,5},{7,6},{8,7},{9,8},{10,9},{11,1... | collective-permute-start | bytes 49160 | tf_op jit(solution)/shard_map/ppermute | solution.py:28
  137.5 6.0 %collective-permute-start.5 = (f32[1,16,256]{2,1,0:T(8,128)S(1)}, f32[1,16,256]{2,1,0:T(8,128)S(1)}, u32[]{:S(2)}, u32[]{:S(2)}) collective-permute-start(f32[1,16,256]{2,1,0:T(8,128)S(1)} %get-tuple-element.42), channel_id=1, source_target_pairs={{0,1},{1,2},{2,3},{3,4},{4,5},{5,6},{6,7},{7,8},{8,9},{9,10},{10,1... | collective-permute-start | bytes 49160 | tf_op jit(solution)/shard_map/ppermute | solution.py:27
  145.0 4.8 %collective-permute-start.6 = (f32[1,16,256]{2,1,0:T(8,128)S(1)}, f32[1,16,256]{2,1,0:T(8,128)S(1)}, u32[]{:S(2)}, u32[]{:S(2)}) collective-permute-start(f32[1,16,256]{2,1,0:T(8,128)S(1)} %get-tuple-element.37), channel_id=1, source_target_pairs={{1,0},{2,1},{3,2},{4,3},{5,4},{6,5},{7,6},{8,7},{9,8},{10,9},{11,1... | collective-permute-start | bytes 49160 | tf_op jit(solution)/shard_map/ppermute | solution.py:28
  146.9 6.0 %collective-permute-start.7 = (f32[1,16,256]{2,1,0:T(8,128)S(1)}, f32[1,16,256]{2,1,0:T(8,128)S(1)}, u32[]{:S(2)}, u32[]{:S(2)}) collective-permute-start(f32[1,16,256]{2,1,0:T(8,128)S(1)} %get-tuple-element.38), channel_id=1, source_target_pairs={{0,1},{1,2},{2,3},{3,4},{4,5},{5,6},{6,7},{7,8},{8,9},{9,10},{10,1... | collective-permute-start | bytes 49160 | tf_op jit(solution)/shard_map/ppermute | solution.py:27
  156.5 29.3 %copy-start.5 = (f32[513,256]{0,1:T(8,128)S(1)}, f32[513,256]{0,1:T(8,128)}, u32[]{:S(2)}) copy-start(f32[513,256]{0,1:T(8,128)} %copy-done.4) | copy-start | bytes 1575940
  265.1 4.7 %collective-permute-start.8 = (f32[1,16,256]{2,1,0:T(8,128)S(1)}, f32[1,16,256]{2,1,0:T(8,128)S(1)}, u32[]{:S(2)}, u32[]{:S(2)}) collective-permute-start(f32[1,16,256]{2,1,0:T(8,128)S(1)} %get-tuple-element.35), channel_id=1, source_target_pairs={{1,0},{2,1},{3,2},{4,3},{5,4},{6,5},{7,6},{8,7},{9,8},{10,9},{11,1... | collective-permute-start | bytes 49160 | tf_op jit(solution)/shard_map/ppermute | solution.py:28
  267.9 6.0 %collective-permute-start.9 = (f32[1,16,256]{2,1,0:T(8,128)S(1)}, f32[1,16,256]{2,1,0:T(8,128)S(1)}, u32[]{:S(2)}, u32[]{:S(2)}) collective-permute-start(f32[1,16,256]{2,1,0:T(8,128)S(1)} %get-tuple-element.36), channel_id=1, source_target_pairs={{0,1},{1,2},{2,3},{3,4},{4,5},{5,6},{6,7},{7,8},{8,9},{9,10},{10,1... | collective-permute-start | bytes 49160 | tf_op jit(solution)/shard_map/ppermute | solution.py:27
  275.4 4.8 %collective-permute-start.10 = (f32[1,16,256]{2,1,0:T(8,128)S(1)}, f32[1,16,256]{2,1,0:T(8,128)S(1)}, u32[]{:S(2)}, u32[]{:S(2)}) collective-permute-start(f32[1,16,256]{2,1,0:T(8,128)S(1)} %get-tuple-element.31), channel_id=1, source_target_pairs={{1,0},{2,1},{3,2},{4,3},{5,4},{6,5},{7,6},{8,7},{9,8},{10,9},{11,1... | collective-permute-start | bytes 49160 | tf_op jit(solution)/shard_map/ppermute | solution.py:28
  277.4 6.0 %collective-permute-start.11 = (f32[1,16,256]{2,1,0:T(8,128)S(1)}, f32[1,16,256]{2,1,0:T(8,128)S(1)}, u32[]{:S(2)}, u32[]{:S(2)}) collective-permute-start(f32[1,16,256]{2,1,0:T(8,128)S(1)} %get-tuple-element.32), channel_id=1, source_target_pairs={{0,1},{1,2},{2,3},{3,4},{4,5},{5,6},{6,7},{7,8},{8,9},{9,10},{10,1... | collective-permute-start | bytes 49160 | tf_op jit(solution)/shard_map/ppermute | solution.py:27
  284.3 4.3 %collective-permute-start.12 = (f32[1,16,256]{2,1,0:T(8,128)S(1)}, f32[1,16,256]{2,1,0:T(8,128)S(1)}, u32[]{:S(2)}, u32[]{:S(2)}) collective-permute-start(f32[1,16,256]{2,1,0:T(8,128)S(1)} %get-tuple-element.29), channel_id=1, source_target_pairs={{1,0},{2,1},{3,2},{4,3},{5,4},{6,5},{7,6},{8,7},{9,8},{10,9},{11,1... | collective-permute-start | bytes 49160 | tf_op jit(solution)/shard_map/ppermute | solution.py:28
  286.2 6.0 %collective-permute-start.13 = (f32[1,16,256]{2,1,0:T(8,128)S(1)}, f32[1,16,256]{2,1,0:T(8,128)S(1)}, u32[]{:S(2)}, u32[]{:S(2)}) collective-permute-start(f32[1,16,256]{2,1,0:T(8,128)S(1)} %get-tuple-element.30), channel_id=1, source_target_pairs={{0,1},{1,2},{2,3},{3,4},{4,5},{5,6},{6,7},{7,8},{8,9},{9,10},{10,1... | collective-permute-start | bytes 49160 | tf_op jit(solution)/shard_map/ppermute | solution.py:27
  293.7 4.8 %collective-permute-start.14 = (f32[1,16,256]{2,1,0:T(8,128)S(1)}, f32[1,16,256]{2,1,0:T(8,128)S(1)}, u32[]{:S(2)}, u32[]{:S(2)}) collective-permute-start(f32[1,16,256]{2,1,0:T(8,128)S(1)} %get-tuple-element.25), channel_id=1, source_target_pairs={{1,0},{2,1},{3,2},{4,3},{5,4},{6,5},{7,6},{8,7},{9,8},{10,9},{11,1... | collective-permute-start | bytes 49160 | tf_op jit(solution)/shard_map/ppermute | solution.py:28
  295.7 6.0 %collective-permute-start.15 = (f32[1,16,256]{2,1,0:T(8,128)S(1)}, f32[1,16,256]{2,1,0:T(8,128)S(1)}, u32[]{:S(2)}, u32[]{:S(2)}) collective-permute-start(f32[1,16,256]{2,1,0:T(8,128)S(1)} %get-tuple-element.26), channel_id=1, source_target_pairs={{0,1},{1,2},{2,3},{3,4},{4,5},{5,6},{6,7},{7,8},{8,9},{9,10},{10,1... | collective-permute-start | bytes 49160 | tf_op jit(solution)/shard_map/ppermute | solution.py:27
where the time goes:
time: 307 us; the launch traced here: 304 us
  matrix products  103 us (34%)
  waiting for transfers between devices  75.1 us (24%)
  blocking collectives  58.8 us (19%)
  starting transfers between devices  46.7 us (15%)
  other arithmetic  14.8 us (5%)
  local copies, waits for them, and re-layouts  4.73 us (2%)
    all_to_all x1, blocking collectives, local(): lax.all_to_all(merged, 'gy', split_axis=0, concat_axis=1, tiled=True)  29.5 us
    all_to_all x1, blocking collectives, local(): lax.all_to_all(jnp.dot(current, forward_z, precision=highest), 'gy', spli...  29.2 us
    ppermute x8, waiting for transfers between devices, extended(): before = lax.ppermute(last, axis, up)  27.1 us
    all_to_all x1, waiting for transfers between devices, local(): lax.all_to_all(merged, 'gy', split_axis=0, concat_axis=1, tiled=True)  25.1 us
    dot_general x2, matrix products, x_inverse(): jnp.dot(sin_back, flat_imag, precision=highest)  24.8 us
    dot_general x2, matrix products, x_inverse(): jnp.dot(cos_back, flat_real, precision=highest)  24.4 us
    all_to_all x1, waiting for transfers between devices, local(): lax.all_to_all(packed, 'gy', split_axis=1, concat_axis=0, tiled=True)  22.8 us
    dot_general x2, matrix products, x_forward(): imag_part = jnp.dot(sin_table, flat, precision=highest).reshape(shape_out)  21.4 us
  transfers between devices with their start and end apart: 18, of which 10 were waited for; matrix products, arithmetic and copies ran while one was open for 1% of the time, Pallas kernels for 0%

commit v1 on v0

v1 whole, which is shorter than its diff:
```python
import functools
import math

import jax
import jax.numpy as jnp
import numpy as np
from jax import lax
from jax.experimental import pallas as pl
from jax.experimental.pallas import tpu as pltpu
from jax.sharding import PartitionSpec as P

OUTER = 2
PASSES = 2
HALO = 8

step_dual = 0.14
step_primal = 0.14
huber_eps = 0.05
bound_dual = 0.5
MESH = pl.DeviceIdType.MESH
f32 = jnp.float32
bf16 = jnp.bfloat16


def split(value):
    high = value.astype(bf16)
    low = (value - high.astype(f32)).astype(bf16)
    return high, low


def dot3(a_high, a_low, b_high, b_low):
    dot = functools.partial(jnp.dot, preferred_element_type=f32)
    return dot(a_high, b_high) + (dot(a_high, b_low) + dot(a_low, b_high))


def kernel(
    n, chunks, part, block,
    cells_ref, table_ref, tilt_ref, wedge_ref, cos_ref, sin_ref, cas_ref, case_ref, zh_ref, zl_ref,
    out_ref,
    gathered, total, data_term, prior_gain, x_high, x_low, m_high, m_low, back,
    target, field, lead, dual_x, dual_y, dual_z, current, code,
    send_sem, recv_sem, back_send, back_recv, halo_send, halo_recv,
):
    me = lax.axis_index("gy")
    ny, rows, nz = cells_ref.shape
    nx = n * rows
    wide = rows + 2 * HALO
    half = n // 2
    row_blocks = nx // block
    chunk_rows = n * part

    barrier = pltpu.get_barrier_semaphore()

    def greet(o, carry):
        pl.semaphore_signal(
            barrier, inc=1, device_id={"gy": lax.rem(me + o, n)}, device_id_type=MESH
        )
        return carry

    lax.fori_loop(1, n, greet, 0)
    pl.semaphore_wait(barrier, n - 1)

    def far(k):
        return (1 - me // half) * half + lax.rem(me + k, half)

    def near(k):
        return (me // half) * half + lax.rem(me + k, half)

    def each_peer(action):
        def first(k, carry):
            action(far(k))
            return carry

        def second(k, carry):
            action(near(k))
            return carry

        lax.fori_loop(0, half, first, 0)
        lax.fori_loop(1, half, second, 0)

    def forward_copy(source, c, peer, owner):
        return pltpu.make_async_remote_copy(
            src_ref=source.at[peer, pl.ds(c * part, part), :],
            dst_ref=gathered.at[c, pl.ds(pl.multiple_of(owner * part, part), part), :],
            send_sem=send_sem.at[c, peer],
            recv_sem=recv_sem.at[c, owner],
            device_id={"gy": peer},
            device_id_type=MESH,
        )

    def back_copy(c, peer, owner):
        return pltpu.make_async_remote_copy(
            src_ref=back.at[c, pl.ds(pl.multiple_of(peer * part, part), part), :],
            dst_ref=target.at[owner, pl.ds(HALO + c * part, part), :],
            send_sem=back_send.at[c, peer],
            recv_sem=back_recv.at[c, owner],
            device_id={"gy": peer},
            device_id_type=MESH,
        )

    def send_forward(source):
        for c in range(chunks):
            each_peer(lambda peer: forward_copy(source, c, peer, me).start())
            gathered[c, pl.ds(pl.multiple_of(me * part, part), part), :] = source[
                me, pl.ds(c * part, part), :
            ]

    def make_tables():
        def group(m, carry):
            lines = (
                cos_ref[pl.ds(m, 1), :] * cas_ref[...] + sin_ref[pl.ds(m, 1), :] * case_ref[...]
            )
            high, low = split(lines)
            at = pl.ds(pl.multiple_of(m * part, part), part)
            x_high[at, :] = high
            x_low[at, :] = low
            return carry

        lax.fori_loop(0, nx // part, group, 0)

    def make_filter():
        lines, columns = tilt_ref.shape
        code[...] = jnp.zeros_like(code)
        code[0:lines, 0:columns] = jnp.where(wedge_ref[...] == 0, 0, tilt_ref[...] + 1).astype(f32)
        depth, width = code.shape
        kz = lax.broadcasted_iota(jnp.int32, (width, nz), 1)
        pick_z = jnp.where(
            lax.broadcasted_iota(jnp.int32, (width, nz), 0) == jnp.minimum(kz, nz - kz), 1.0, 0.0
        ).astype(bf16)
        spread = jnp.dot(code[...].astype(bf16), pick_z, preferred_element_type=f32).astype(bf16)

        def body(b, carry):
            line = b * block + lax.broadcasted_iota(jnp.int32, (block, depth), 0)
            c = line // chunk_rows
            owner = (line % chunk_rows) // part
            kx = owner * rows + c * part + line % part
            column = lax.broadcasted_iota(jnp.int32, (block, depth), 1)
            pick_x = jnp.where(column == jnp.minimum(kx, nx - kx), 1.0, 0.0).astype(bf16)
            which = jnp.dot(pick_x, spread, preferred_element_type=f32)
            response = jnp.zeros_like(which)
            for level in range(table_ref.shape[0]):
                response = jnp.where(which == level + 1.0, table_ref[level], response)
            prior = 1.0 / (response * response + 1.0)
            at = pl.ds(pl.multiple_of(b * block, block), block)
            prior_gain[at, :] = prior
            data_term[at, :] = response * prior
            return carry

        lax.fori_loop(0, row_blocks, body, 0)

    def x_forward():
        for c in range(chunks):
            def arrived(o, carry):
                owner = lax.rem(me + o, n)
                forward_copy(current, c, owner, owner).wait_recv()
                return carry

            lax.fori_loop(1, n, arrived, 0)
            high, low = split(gathered[c])

            def body(b, carry):
                at = pl.ds(pl.multiple_of(b * block, block), block)
                span = pl.ds(c * chunk_rows, chunk_rows)
                product = dot3(x_high[at, span], x_low[at, span], high, low)
                if c == 0:
                    total[at, :] = product
                else:
                    total[at, :] += product
                return carry

            lax.fori_loop(0, row_blocks, body, 0)

    def mix(outer):
        def body(b, carry):
            at = pl.ds(pl.multiple_of(b * block, block), block)
            high, low = split(total[at, :])
            spectrum = dot3(high, low, zh_ref[...], zl_ref[...])
            if outer == 0:
                data_term[at, :] = data_term[at, :] * spectrum
            mixed = data_term[at, :] + prior_gain[at, :] * spectrum
            high, low = split(mixed)
            high, low = split(dot3(high, low, zh_ref[...], zl_ref[...]))
            m_high[at, :] = high
            m_low[at, :] = low
            return carry

        lax.fori_loop(0, row_blocks, body, 0)

    order = [0] + ([chunks - 1] if chunks > 1 else []) + list(range(1, chunks - 1))
    before, after = lax.rem(me + n - 1, n), lax.rem(me + 1, n)

    def halo_up():
        return pltpu.make_async_remote_copy(
            src_ref=target.at[:, pl.ds(rows, HALO), :],
            dst_ref=target.at[:, pl.ds(0, HALO), :],
            send_sem=halo_send.at[0],
            recv_sem=halo_recv.at[0],
            device_id={"gy": after},
            device_id_type=MESH,
        )

    def halo_down():
        return pltpu.make_async_remote_copy(
            src_ref=target.at[:, pl.ds(HALO, HALO), :],
            dst_ref=target.at[:, pl.ds(HALO + rows, HALO), :],
            send_sem=halo_send.at[1],
            recv_sem=halo_recv.at[1],
            device_id={"gy": before},
            device_id_type=MESH,
        )

    def x_backward():
        for c in order:
            span = pl.ds(c * chunk_rows, chunk_rows)
            step = min(block, chunk_rows)

            def body(b, carry):
                at = pl.ds(pl.multiple_of(b * step, step), step)
                line = pl.ds(pl.multiple_of(c * chunk_rows + b * step, step), step)
                back[c, at, :] = dot3(x_high[line, :], x_low[line, :], m_high[...], m_low[...])
                return carry

            lax.fori_loop(0, chunk_rows // step, body, 0)
            each_peer(lambda peer: back_copy(c, peer, me).start())
            target[me, pl.ds(HALO + c * part, part), :] = back[
                c, pl.ds(pl.multiple_of(me * part, part), part), :
            ]
        for c in order:
            def arrived(o, carry):
                owner = lax.rem(me + o, n)
                back_copy(c, owner, owner).wait_recv()
                return carry

            lax.fori_loop(1, n, arrived, 0)
            if c == order[0]:
                @pl.when(me > 0)
                def _():
                    halo_down().start()
            if c == chunks - 1:
                @pl.when(me < n - 1)
                def _():
                    halo_up().start()

        @pl.when(me > 0)
        def _():
            halo_up().wait_recv()
            halo_down().wait_send()

        @pl.when(me < n - 1)
        def _():
            halo_down().wait_recv()
            halo_up().wait_send()

        def sent(o, carry):
            for c in range(chunks):
                back_copy(c, lax.rem(me + o, n), me).wait_send()
            return carry

        lax.fori_loop(1, n, sent, 0)

    def wait_forward_sent(source):
        def sent(o, carry):
            for c in range(chunks):
                forward_copy(source, c, lax.rem(me + o, n), me).wait_send()
            return carry

        lax.fori_loop(1, n, sent, 0)

    def denoise(outer):
        column = lax.broadcasted_iota(jnp.int32, (wide, nz), 1)
        line = lax.broadcasted_iota(jnp.int32, (wide, nz), 0) + (me * rows - HALO)
        inside = jnp.where((line >= 0) & (line < nx), 1.0, 0.0)
        not_first = jnp.where(column > 0, 1.0, 0.0)
        not_last = jnp.where(column < nz - 1, 1.0, 0.0)

        def bend_x(value):
            return pltpu.roll(value, 1, 0) + pltpu.roll(value, wide - 1, 0) - 2.0 * value

        def bend_z(value):
            return (
                pltpu.roll(value, 1, 1) * not_first
                + pltpu.roll(value, nz - 1, 1) * not_last
                - 2.0 * value
            )

        def neighbours(ref, y):
            low = ref[jnp.maximum(y - 1, 0)] * jnp.where(y > 0, 1.0, 0.0)
            high = ref[jnp.minimum(y + 1, ny - 1)] * jnp.where(y < ny - 1, 1.0, 0.0)
            return low + high - 2.0 * ref[y]

        scale = 1.0 / (1.0 + step_dual * huber_eps / bound_dual)
        for sweep in range(PASSES):
            origin = target if sweep == 0 else lead
            base = target if sweep == 0 else field
            fresh = outer == 0 and sweep == 0

            def rise(y):
                here = origin[y]
                bends = (bend_x(here), neighbours(origin, y), bend_z(here))
                if fresh:
                    raised = [bend * (step_dual * scale) for bend in bends]
                else:
                    raised = [
                        dual[y] * scale + bend * (step_dual * scale)
                        for dual, bend in zip((dual_x, dual_y, dual_z), bends)
                    ]
                norm = raised[0] * raised[0] + raised[1] * raised[1] + raised[2] * raised[2]
                shrink = lax.rsqrt(jnp.maximum(1.0, norm * (1.0 / bound_dual**2))) * inside
                dual_x[y] = raised[0] * shrink
                dual_y[y] = raised[1] * shrink
                dual_z[y] = raised[2] * shrink

            def fall(y):
                adjoint = bend_x(dual_x[y]) + neighbours(dual_y, y) + bend_z(dual_z[y])
                old = base[y]
                updated = (
                    (old - step_primal * adjoint + step_primal * target[y])
                    * (1.0 / (1.0 + step_primal))
                    * inside
                )
                if sweep < PASSES - 1:
                    lead[y] = 2.0 * updated - old
                    field[y] = updated
                elif outer < OUTER - 1:
                    current[y] = updated[HALO : HALO + rows, :]
                else:
                    out_ref[y] = updated[HALO : HALO + rows, :]

            rise(0)

            def body(y, carry):
                rise(y)
                fall(y - 1)
                return carry

            lax.fori_loop(1, ny, body, 0)
            fall(ny - 1)

    send_forward(cells_ref)

    @pl.when(me == 0)
    def _():
        target[:, 0:HALO, :] = jnp.zeros((ny, HALO, nz), f32)

    @pl.when(me == n - 1)
    def _():
        target[:, rows + HALO : wide, :] = jnp.zeros((ny, HALO, nz), f32)

    make_tables()
    make_filter()
    for outer in range(OUTER):
        x_forward()
        mix(outer)
        wait_forward_sent(cells_ref if outer == 0 else current)
        x_backward()
        denoise(outer)
        if outer < OUTER - 1:
            send_forward(current)


def constants(n, rows, part, nz):
    nx = n * rows
    line = np.arange(nx)
    place = (line % (n * part)) // part * rows + line // (n * part) * part + line % part
    turn = 2.0 * math.pi / nx
    starts = place[::part]
    coarse = (starts[:, None] * place[None, :] % nx) * turn
    fine = (np.arange(part)[:, None] * place[None, :] % nx) * turn
    norm = 1.0 / math.sqrt(nx)
    tables = (
        np.cos(coarse),
        np.sin(coarse),
        (np.cos(fine) + np.sin(fine)) * norm,
        (np.cos(fine) - np.sin(fine)) * norm,
    )
    k = np.arange(nz)
    angle = (k[:, None] * k[None, :] % nz) * (2.0 * math.pi / nz)
    cas_z = ((np.cos(angle) + np.sin(angle)) / math.sqrt(nz)).astype(np.float32)
    z_high = cas_z.astype(bf16)
    z_low = (cas_z - z_high.astype(np.float32)).astype(bf16)
    return [jnp.asarray(t, f32) for t in tables] + [jnp.asarray(z_high), jnp.asarray(z_low)]


def local(n, observed, tf_table, tilt_index, wedge):
    rows, ny, nz = observed.shape
    nx = n * rows
    part = rows // 4 if rows % 32 == 0 else rows
    chunks = rows // part
    block = min(nx, 256)
    wide = rows + 2 * HALO
    lines, columns = tilt_index.shape
    depth, width = -(-lines // 128) * 128, -(-columns // 128) * 128
    tables = constants(n, rows, part, nz)
    vmem = pl.BlockSpec(memory_space=pltpu.VMEM)
    smem = pl.BlockSpec(memory_space=pltpu.SMEM)
    slab = pltpu.VMEM((ny, wide, nz), f32)
    plane = pltpu.VMEM((nx, nz), f32)
    result = pl.pallas_call(
        functools.partial(kernel, n, chunks, part, block),
        out_shape=jax.ShapeDtypeStruct((ny, rows, nz), f32),
        in_specs=[vmem, smem] + [vmem] * 8,
        out_specs=vmem,
        scratch_shapes=[
            pltpu.VMEM((chunks, n * part, nz), f32),
            plane,
            plane,
            plane,
            pltpu.VMEM((nx, nx), bf16),
            pltpu.VMEM((nx, nx), bf16),
            pltpu.VMEM((nx, nz), bf16),
            pltpu.VMEM((nx, nz), bf16),
            pltpu.VMEM((chunks, n * part, nz), f32),
            slab,
            slab,
            slab,
            slab,
            slab,
            slab,
            pltpu.VMEM((ny, rows, nz), f32),
            pltpu.VMEM((depth, width), f32),
            pltpu.SemaphoreType.DMA((chunks, n)),
            pltpu.SemaphoreType.DMA((chunks, n)),
            pltpu.SemaphoreType.DMA((chunks, n)),
            pltpu.SemaphoreType.DMA((chunks, n)),
            pltpu.SemaphoreType.DMA((2,)),
            pltpu.SemaphoreType.DMA((2,)),
        ],
        compiler_params=pltpu.CompilerParams(
            collective_id=0, has_side_effects=True, vmem_limit_bytes=60 * 1024 * 1024
        ),
    )(jnp.swapaxes(observed, 0, 1), tf_table, tilt_index, wedge, *tables)
    return jnp.swapaxes(result, 0, 1)


def solution(mesh):
    in_specs = (P(("groups", "gy"), None, None), P(), P(), P())
    out_specs = P(("groups", "gy"), None, None)
    body = functools.partial(local, mesh.shape["gy"])
    return jax.shard_map(body, mesh=mesh, in_specs=in_specs, out_specs=out_specs, check_vma=False)
```

time: 307 us -> 144 us (0.47)
  Pallas kernels: 0 us -> 134 us
  matrix products: 103 us -> 0 us
  waiting for transfers between devices: 75.1 us -> 0 us
  blocking collectives: 58.8 us -> 0 us
  starting transfers between devices: 46.7 us -> 0 us
  other arithmetic: 14.8 us -> 0 us
    pallas_call x0 -> x1, Pallas kernels: none -> 134 us  [local(): pl.pallas_call(functools.partial(kernel, n, chunks, part, block), out_sha...]
    dot_general x12 -> x0, matrix products: 103 us -> none  [the longest x2 24.8 us: x_inverse(): jnp.dot(sin_back, flat_imag, precision=highest)]
    all_to_all x2 -> x0, blocking collectives: 58.8 us -> none  [the longest x1 29.5 us: local(): lax.all_to_all(merged, 'gy', split_axis=0, concat_axis=1, tiled=True)]
    all_to_all x2 -> x0, waiting for transfers between devices: 47.9 us -> none  [the longest x1 25.1 us: local(): lax.all_to_all(merged, 'gy', split_axis=0, concat_axis=1, tiled=True)]
    ppermute x16 -> x0, starting transfers between devices: 35.4 us -> none  [the longest x8 18.3 us: extended(): before = lax.ppermute(last, axis, up)]
    ppermute x16 -> x0, waiting for transfers between devices: 27.1 us -> none  [the longest x8 27.1 us: extended(): before = lax.ppermute(last, axis, up)]
    all_to_all x2 -> x0, starting transfers between devices: 11.3 us -> none  [the longest x1 6.76 us: local(): lax.all_to_all(packed, 'gy', split_axis=1, concat_axis=0, tiled=True)]
    div x12 -> x0, other arithmetic: 11 us -> none  [the longest x8 8.02 us: denoise(): duals = (raised[0] / shrink, raised[1] / shrink, raised[2] / shrink)]
  transfers between devices with their start and end apart: 18 -> 0, of which waited for: 10 -> 0; matrix products, arithmetic and copies ran while one was open for 1% -> 0% of each run, Pallas kernels for 0% -> 0%
where the time goes in v1:
time: 144 us; the launch traced here: 142 us
  Pallas kernels  134 us (93%)
  local copies, waits for them, and re-layouts  7.5 us (5%)
    pallas_call x1, Pallas kernels, local(): pl.pallas_call(functools.partial(kernel, n, chunks, part, block), out_sha...  134 us
    unnamed x7, local copies, waits for them, and re-layouts  4.69 us

profile of v1, /device:TPU:16, one launch (start us, length us, event | category | flops | bytes accessed | tf_op | source)
XLA Modules:
  0.0 141.9 jit_solution(3198146938334129781)
XLA Ops:
  0.0 0.0 copy-start.1
  0.0 0.0 copy-start
  0.0 2.1 %copy.12.tilt_ref = s32[513,129]{1,0:T(8,128)} copy(s32[513,129]{0,1:T(8,128)} %param.12) | data formatting | bytes 529416 | tf_op args[2]
  2.1 0.0 copy-done.1
  2.1 1.0 copy.13.wedge_ref
  3.1 0.0 copy-done
  3.1 1.6 %copy.16 = f32[64,16,256]{2,0,1:T(8,128)} copy(f32[64,16,256]{2,1,0:T(8,128)S(1)} %copy-done) | data formatting | bytes 2097152 | tf_op args[0]
  4.7 134.4 %shard_map.100 = f32[16,64,256]{2,1,0:T(8,128)} custom-call(f32[16,64,256]{2,1,0:T(8,128)} %bitcast.5, f32[16]{0:T(128)} %table_ref.1, s32[513,129]{1,0:T(8,128)} %copy.12.tilt_ref, s32[513,129]{1,0:T(8,128)} %copy.13.wedge_ref, f32[64,1024]{1,0:T(8,128)} %constant.12.clone.cos_ref, f32[64,1024]{1,0:T(8,128)} %constant.13.clone.sin_ref, ...), custom_call_target="tpu_custom_call" | custom-call | tf_op jit(solution)/shard_map/pallas_call | solution.py:398
  139.1 2.8 %copy.14 = f32[64,16,256]{2,1,0:T(8,128)} copy(f32[64,16,256]{2,0,1:T(8,128)} %bitcast.4) | data formatting | bytes 2097152 | tf_op jit(solution)/shard_map/transpose | solution.py:432
Async XLA Ops:
  0.0 2.1 %copy-start.1 = (s32[513,129]{0,1:T(8,128)S(1)}, s32[513,129]{0,1:T(8,128)}, u32[]{:S(2)}) copy-start(s32[513,129]{0,1:T(8,128)} %param.13) | copy-start | bytes 794128
  0.0 3.1 %copy-start = (f32[64,16,256]{2,1,0:T(8,128)S(1)}, f32[64,16,256]{2,1,0:T(8,128)}, u32[]{:S(2)}) copy-start(f32[64,16,256]{2,1,0:T(8,128)} %param.10) | copy-start | bytes 3145732

commit v2 on v1

v2 whole, which is shorter than its diff:
```python
import functools
import math

import jax
import jax.numpy as jnp
import numpy as np
from jax import lax
from jax.experimental import pallas as pl
from jax.experimental.pallas import tpu as pltpu
from jax.sharding import PartitionSpec as P

OUTER = 2
PASSES = 2
GROUP = 8
LANES = 128

step_dual = 0.14
step_primal = 0.14
huber_eps = 0.05
bound_dual = 0.5
MESH = pl.DeviceIdType.MESH
f32 = jnp.float32
bf16 = jnp.bfloat16


def split(value):
    high = value.astype(bf16)
    low = (value - high.astype(f32)).astype(bf16)
    return high, low


def dot3(a_high, a_low, b_high, b_low):
    dot = functools.partial(jnp.dot, preferred_element_type=f32)
    return dot(a_high, b_high) + (dot(a_high, b_low) + dot(a_low, b_high))


def kernel(
    n, rows, order,
    cells_ref, table_ref, tilt_ref, wedge_ref, cos_ref, sin_ref, cas_ref, case_ref, zh_ref, zl_ref,
    out_ref,
    gathered, total, data_term, prior_gain, x_high, x_low, m_high, m_low, back,
    target, halo, field, lead, duals, current, code,
    send_sem, recv_sem, back_send, back_recv, halo_send, halo_recv,
):
    me = lax.axis_index("gy")
    chunks, slots = len(order), len(order[0])
    groups = chunks * slots
    seat = {g: (c, s) for c in range(chunks) for s, g in enumerate(order[c])}
    part = slots * GROUP
    ny, nz = out_ref.shape[0], out_ref.shape[2]
    nx = n * rows
    half = n // 2
    span_rows = n * part
    block = math.gcd(nx, 256)
    row_blocks = nx // block

    barrier = pltpu.get_barrier_semaphore()

    def greet(o, carry):
        pl.semaphore_signal(
            barrier, inc=1, device_id={"gy": lax.rem(me + o, n)}, device_id_type=MESH
        )
        return carry

    lax.fori_loop(1, n, greet, 0)

    def each_peer(action):
        def first(k, carry):
            action((1 - me // half) * half + lax.rem(me + k, half))
            return carry

        def second(k, carry):
            action((me // half) * half + lax.rem(me + k, half))
            return carry

        lax.fori_loop(0, half, first, 0)
        lax.fori_loop(1, half, second, 0)

    def every_other(action):
        def step(o, carry):
            action(lax.rem(me + o, n))
            return carry

        lax.fori_loop(1, n, step, 0)

    def forward_copy(c, peer, owner):
        return pltpu.make_async_remote_copy(
            src_ref=current.at[peer, c],
            dst_ref=gathered.at[c, owner],
            send_sem=send_sem.at[c, peer],
            recv_sem=recv_sem.at[c, owner],
            device_id={"gy": peer},
            device_id_type=MESH,
        )

    def back_copy(c, peer, owner):
        return pltpu.make_async_remote_copy(
            src_ref=back.at[c, peer],
            dst_ref=target.at[owner, c],
            send_sem=back_send.at[c, peer],
            recv_sem=back_recv.at[c, owner],
            device_id={"gy": peer},
            device_id_type=MESH,
        )

    def halo_copy(side):
        return pltpu.make_async_remote_copy(
            src_ref=target.at[:, 0, slots - 1 if side == 0 else 0],
            dst_ref=halo.at[side],
            send_sem=halo_send.at[side],
            recv_sem=halo_recv.at[side],
            device_id={"gy": lax.rem(me + (1 if side == 0 else n - 1), n)},
            device_id_type=MESH,
        )

    def send_forward(c):
        each_peer(lambda peer: forward_copy(c, peer, me).start())
        gathered[c, me] = current[me, c]

    def stage(y, carry):
        stride = ny * nz // LANES
        for z in range(nz // LANES):
            first = (y // GROUP * (nz // LANES) + z) * GROUP + y % GROUP
            lines = cells_ref[pl.ds(first, rows, stride=stride), :]
            for g, (c, s) in seat.items():
                current[y, c, s, :, z * LANES : (z + 1) * LANES] = lines[
                    g * GROUP : (g + 1) * GROUP, :
                ]
        return carry

    def make_tables():
        def body(m, carry):
            lines = jnp.concatenate(
                [
                    cos_ref[pl.ds(k, 1), :] * cas_ref[...] + sin_ref[pl.ds(k, 1), :] * case_ref[...]
                    for k in (2 * m, 2 * m + 1)
                ],
                axis=0,
            )
            at = pl.ds(pl.multiple_of(m * 2 * GROUP, 2 * GROUP), 2 * GROUP)
            x_high[at, :], x_low[at, :] = split(lines)
            return carry

        lax.fori_loop(0, nx // (2 * GROUP), body, 0)

    def make_filter():
        columns, lines = tilt_ref.shape
        code[...] = jnp.zeros_like(code)
        code[0:columns, 0:lines] = jnp.where(wedge_ref[...] == 0, 0, tilt_ref[...] + 1).astype(f32)
        width, depth = code.shape
        kz = lax.broadcasted_iota(jnp.int32, (nz, width), 0)
        pick_z = jnp.where(
            lax.broadcasted_iota(jnp.int32, (nz, width), 1) == jnp.minimum(kz, nz - kz), 1.0, 0.0
        ).astype(bf16)
        spread = jnp.dot(pick_z, code[...].astype(bf16), preferred_element_type=f32).astype(bf16)

        def body(b, carry):
            line = b * block + lax.broadcasted_iota(jnp.int32, (block, depth), 0)
            c = line // span_rows
            slot = line % part // GROUP
            group = slot if chunks == 1 else jnp.where(slot == 0, c, groups - 1 - c)
            kx = line % span_rows // part * rows + group * GROUP + line % GROUP
            column = lax.broadcasted_iota(jnp.int32, (block, depth), 1)
            pick_x = jnp.where(column == jnp.minimum(kx, nx - kx), 1.0, 0.0).astype(bf16)
            which = lax.dot_general(
                pick_x, spread, (((1,), (1,)), ((), ())), preferred_element_type=f32
            )
            response = jnp.zeros_like(which)
            for level in range(table_ref.shape[0]):
                response = jnp.where(which == level + 1.0, table_ref[level], response)
            prior = 1.0 / (response * response + 1.0)
            at = pl.ds(pl.multiple_of(b * block, block), block)
            prior_gain[at, :] = prior
            data_term[at, :] = response * prior
            return carry

        lax.fori_loop(0, row_blocks, body, 0)

    def filtered(outer):
        for c in range(chunks):
            every_other(lambda owner: forward_copy(c, owner, owner).wait_recv())
            high, low = split(gathered[c].reshape(span_rows, nz))
            high, low = split(dot3(high, low, zh_ref[...], zl_ref[...]))

            def body(b, carry):
                at = pl.ds(pl.multiple_of(b * block, block), block)
                span = pl.ds(c * span_rows, span_rows)
                spectrum = dot3(x_high[at, span], x_low[at, span], high, low)
                if c > 0:
                    spectrum = total[at, :] + spectrum
                if c < chunks - 1:
                    total[at, :] = spectrum
                    return carry
                if outer == 0:
                    data_term[at, :] = data_term[at, :] * spectrum
                a_high, a_low = split(data_term[at, :] + prior_gain[at, :] * spectrum)
                m_high[at, :], m_low[at, :] = split(dot3(a_high, a_low, zh_ref[...], zl_ref[...]))
                return carry

            lax.fori_loop(0, row_blocks, body, 0)

    def send_back(c):
        step = math.gcd(span_rows, 256)

        def body(b, carry):
            line = pl.ds(pl.multiple_of(c * span_rows + b * step, step), step)
            lines = dot3(x_high[line, :], x_low[line, :], m_high[...], m_low[...])
            count = step // part
            at = pl.ds(pl.multiple_of(b * count, count), count)
            back[c, at] = lines.reshape(count, slots, GROUP, nz)
            return carry

        lax.fori_loop(0, span_rows // step, body, 0)
        each_peer(lambda peer: back_copy(c, peer, me).start())
        target[me, c] = back[c, me]

    def denoise(outer, index, low, high):
        dual_x, dual_y, dual_z = duals[3 * index : 3 * index + 3]
        wide = (high - low + 2) * GROUP
        column = lax.broadcasted_iota(jnp.int32, (wide, nz), 1)
        not_first = jnp.where(column > 0, 1.0, 0.0)
        not_last = jnp.where(column < nz - 1, 1.0, 0.0)
        edge = low == 0 or high == groups
        if edge:
            line = lax.broadcasted_iota(jnp.int32, (wide, nz), 0) + (me * rows + (low - 1) * GROUP)
            inside = jnp.where((line >= 0) & (line < nx), 1.0, 0.0)

        def bend_x(value):
            return pltpu.roll(value, 1, 0) + pltpu.roll(value, wide - 1, 0) - 2.0 * value

        def bend_z(value):
            return (
                pltpu.roll(value, 1, 1) * not_first
                + pltpu.roll(value, nz - 1, 1) * not_last
                - 2.0 * value
            )

        def neighbours(get, y):
            below = get(jnp.maximum(y - 1, 0)) * jnp.where(y > 0, 1.0, 0.0)
            above = get(jnp.minimum(y + 1, ny - 1)) * jnp.where(y < ny - 1, 1.0, 0.0)
            return below + above - 2.0 * get(y)

        def goal(y):
            pieces = []
            for g in range(low - 1, high + 1):
                if g < 0:
                    pieces.append(halo[0, y])
                elif g >= groups:
                    pieces.append(halo[1, y])
                else:
                    pieces.append(target[y, seat[g][0], seat[g][1]])
            return jnp.concatenate(pieces, axis=0)

        def reader(ref):
            return lambda y: ref[y, 0:wide, :]

        scale = 1.0 / (1.0 + step_dual * huber_eps / bound_dual)
        for sweep in range(PASSES):
            origin = goal if sweep == 0 else reader(lead)
            base = goal if sweep == 0 else reader(field)
            fresh = outer == 0 and sweep == 0

            def rise(y):
                here = origin(y)
                bends = (bend_x(here), neighbours(origin, y), bend_z(here))
                if fresh:
                    raised = [bend * (step_dual * scale) for bend in bends]
                else:
                    raised = [
                        dual[y] * scale + bend * (step_dual * scale)
                        for dual, bend in zip((dual_x, dual_y, dual_z), bends)
                    ]
                norm = raised[0] * raised[0] + raised[1] * raised[1] + raised[2] * raised[2]
                shrink = lax.rsqrt(jnp.maximum(1.0, norm * (1.0 / bound_dual**2)))
                if edge:
                    shrink = shrink * inside
                dual_x[y] = raised[0] * shrink
                dual_y[y] = raised[1] * shrink
                dual_z[y] = raised[2] * shrink

            def fall(y):
                adjoint = (
                    bend_x(dual_x[y]) + neighbours(lambda at: dual_y[at], y) + bend_z(dual_z[y])
                )
                old = base(y)
                updated = (old - step_primal * adjoint + step_primal * goal(y)) * (
                    1.0 / (1.0 + step_primal)
                )
                if sweep < PASSES - 1:
                    if edge:
                        updated = updated * inside
                    lead[y, 0:wide, :] = 2.0 * updated - old
                    field[y, 0:wide, :] = updated
                elif outer < OUTER - 1:
                    for g in range(low, high):
                        start = (g - low + 1) * GROUP
                        current[y, seat[g][0], seat[g][1]] = updated[start : start + GROUP, :]
                else:
                    out_ref[y, low * GROUP : high * GROUP, :] = updated[GROUP : wide - GROUP, :]

            rise(0)

            def body(y, carry):
                rise(y)
                fall(y - 1)
                return carry

            lax.fori_loop(1, ny, body, 0)
            fall(ny - 1)

    lax.fori_loop(0, ny, stage, 0)
    pl.semaphore_wait(barrier, n - 1)
    for c in range(chunks):
        send_forward(c)

    @pl.when(me == 0)
    def _():
        halo[0] = jnp.zeros(halo.shape[1:], f32)

    @pl.when(me == n - 1)
    def _():
        halo[1] = jnp.zeros(halo.shape[1:], f32)

    make_tables()
    make_filter()
    quarter = groups // 4
    for outer in range(OUTER):
        filtered(outer)
        for c in range(chunks):
            every_other(lambda peer: forward_copy(c, peer, me).wait_send())
        for c in range(chunks):
            send_back(c)

        def arrive(some):
            for c in some:
                every_other(lambda owner: back_copy(c, owner, owner).wait_recv())

        arrive([0])

        @pl.when(me < n - 1)
        def _():
            halo_copy(0).start()

        @pl.when(me > 0)
        def _():
            halo_copy(1).start()

        early = list(range(1, quarter + 1)) if chunks > 1 else []
        arrive(early)

        @pl.when(me > 0)
        def _():
            halo_copy(0).wait_recv()

        @pl.when(me < n - 1)
        def _():
            halo_copy(1).wait_recv()

        done = 0
        if chunks > 1:
            denoise(outer, 0, 0, quarter)
            denoise(outer, 1, groups - quarter, groups)
            done = quarter
            if outer < OUTER - 1:
                for c in range(done):
                    send_forward(c)
            arrive(range(quarter + 1, chunks))
            denoise(outer, 2, quarter, groups - quarter)
        else:
            denoise(outer, 0, 0, groups)

        @pl.when(me < n - 1)
        def _():
            halo_copy(0).wait_send()

        @pl.when(me > 0)
        def _():
            halo_copy(1).wait_send()

        for c in range(chunks):
            every_other(lambda peer: back_copy(c, peer, me).wait_send())
        if outer < OUTER - 1:
            for c in range(done, chunks):
                send_forward(c)


def constants(n, rows, order, nz):
    nx = n * rows
    place = np.array(
        [
            d * rows + g * GROUP + r
            for some in order
            for d in range(n)
            for g in some
            for r in range(GROUP)
        ]
    )
    turn = 2.0 * math.pi / nx
    coarse = (place[::GROUP, None] * place[None, :] % nx) * turn
    fine = (np.arange(GROUP)[:, None] * place[None, :] % nx) * turn
    norm = 1.0 / math.sqrt(nx)
    tables = (
        np.cos(coarse),
        np.sin(coarse),
        (np.cos(fine) + np.sin(fine)) * norm,
        (np.cos(fine) - np.sin(fine)) * norm,
    )
    k = np.arange(nz)
    angle = (k[:, None] * k[None, :] % nz) * (2.0 * math.pi / nz)
    cas_z = ((np.cos(angle) + np.sin(angle)) / math.sqrt(nz)).astype(np.float32)
    z_high = cas_z.astype(bf16)
    z_low = (cas_z - z_high.astype(np.float32)).astype(bf16)
    return [jnp.asarray(t, f32) for t in tables] + [jnp.asarray(z_high), jnp.asarray(z_low)]


def local(n, observed, tf_table, tilt_index, wedge):
    rows, ny, nz = observed.shape
    nx = n * rows
    groups = rows // GROUP
    if groups % 4 == 0:
        order = [(c, groups - 1 - c) for c in range(groups // 2)]
        sizes = [groups // 4, groups // 4, groups // 2]
    else:
        order = [tuple(range(groups))]
        sizes = [groups]
    chunks, slots = len(order), len(order[0])
    lines, columns = tilt_index.shape
    depth, width = -(-lines // 128) * 128, -(-columns // 128) * 128
    tables = constants(n, rows, order, nz)
    tiles = observed.reshape(rows, ny // GROUP, GROUP, nz // LANES, LANES)
    tiles = tiles.transpose(0, 1, 3, 2, 4).reshape(-1, LANES)
    vmem = pl.BlockSpec(memory_space=pltpu.VMEM)
    smem = pl.BlockSpec(memory_space=pltpu.SMEM)
    tile_rows = [(size + 2) * GROUP for size in sizes]
    scratch_tile = pltpu.VMEM((ny, max(tile_rows), nz), f32)
    plane = pltpu.VMEM((nx, nz), f32)
    blocks = pltpu.VMEM((chunks, n, slots, GROUP, nz), f32)
    cells = pltpu.VMEM((ny, chunks, slots, GROUP, nz), f32)
    semaphores = pltpu.SemaphoreType.DMA((chunks, n))
    result = pl.pallas_call(
        functools.partial(kernel, n, rows, order),
        out_shape=jax.ShapeDtypeStruct((ny, rows, nz), f32),
        in_specs=[vmem, smem] + [vmem] * 8,
        out_specs=vmem,
        scratch_shapes=[
            blocks,
            plane,
            plane,
            plane,
            pltpu.VMEM((nx, nx), bf16),
            pltpu.VMEM((nx, nx), bf16),
            pltpu.VMEM((nx, nz), bf16),
            pltpu.VMEM((nx, nz), bf16),
            blocks,
            cells,
            pltpu.VMEM((2, ny, GROUP, nz), f32),
            scratch_tile,
            scratch_tile,
            [pltpu.VMEM((ny, size, nz), f32) for size in tile_rows for _ in range(3)],
            cells,
            pltpu.VMEM((width, depth), f32),
            semaphores,
            semaphores,
            semaphores,
            semaphores,
            pltpu.SemaphoreType.DMA((2,)),
            pltpu.SemaphoreType.DMA((2,)),
        ],
        compiler_params=pltpu.CompilerParams(
            collective_id=0, has_side_effects=True, vmem_limit_bytes=60 * 1024 * 1024
        ),
    )(tiles, tf_table, tilt_index.T, wedge.T, *tables)
    return jnp.swapaxes(result, 0, 1)


def solution(mesh):
    in_specs = (P(("groups", "gy"), None, None), P(), P(), P())
    out_specs = P(("groups", "gy"), None, None)
    body = functools.partial(local, mesh.shape["gy"])
    return jax.shard_map(body, mesh=mesh, in_specs=in_specs, out_specs=out_specs, check_vma=False)
```

time: 144 us -> 149 us (1.035); the launches traced: 142 us -> 149 us
  Pallas kernels: 134 us -> 146 us
  local copies, waits for them, and re-layouts: 7.5 us -> 2.81 us
    pallas_call x1, Pallas kernels: 134 us -> 146 us  [local(): pl.pallas_call(functools.partial(kernel, n, rows, order), out_shape=jax.S...]
    unnamed x7 -> x0, local copies, waits for them, and re-layouts: 4.69 us -> none
where the time goes in v2:
time: 149 us
  Pallas kernels  146 us (98%)
  local copies, waits for them, and re-layouts  2.81 us (2%)
    pallas_call x1, Pallas kernels, local(): pl.pallas_call(functools.partial(kernel, n, rows, order), out_shape=jax.S...  146 us

profile of v2, /device:TPU:16, one launch (start us, length us, event | category | flops | bytes accessed | tf_op | source)
XLA Modules:
  0.0 148.5 jit_solution(10793895964338505924)
XLA Ops:
  0.0 145.7 %shard_map.100 = f32[16,64,256]{2,1,0:T(8,128)} custom-call(f32[2048,128]{1,0:T(8,128)} %bitcast.9, f32[16]{0:T(128)} %table_ref.1, s32[129,513]{1,0:T(8,128)} %bitcast.10, s32[129,513]{1,0:T(8,128)} %bitcast.11, f32[128,1024]{1,0:T(8,128)} %constant.12.clone.cos_ref, f32[128,1024]{1,0:T(8,128)} %constant.13.clone.sin_ref, ...), custom_call_target="tpu_custom_call" | custom-call | tf_op jit(solution)/shard_map/pallas_call | solution.py:440
  145.7 2.8 %copy.11 = f32[64,16,256]{2,1,0:T(8,128)} copy(f32[64,16,256]{2,0,1:T(8,128)} %bitcast.8) | data formatting | bytes 2097152 | tf_op jit(solution)/shard_map/transpose | solution.py:473

commit v3 on v2

--- a/solution.py
+++ b/solution.py
@@ -18,6 +18,8 @@
 step_primal = 0.14
 huber_eps = 0.05
 bound_dual = 0.5
+relax = 1.0 / (1.0 + step_dual * huber_eps / bound_dual)
+gain = step_dual * relax
 MESH = pl.DeviceIdType.MESH
 f32 = jnp.float32
 bf16 = jnp.bfloat16
@@ -39,7 +41,7 @@
     cells_ref, table_ref, tilt_ref, wedge_ref, cos_ref, sin_ref, cas_ref, case_ref, zh_ref, zl_ref,
     out_ref,
     gathered, total, data_term, prior_gain, x_high, x_low, m_high, m_low, back,
-    target, halo, field, lead, duals, current, code,
+    target, halo, goal, field, lead, duals, current, code,
     send_sem, recv_sem, back_send, back_recv, halo_send, halo_recv,
 ):
     me = lax.axis_index("gy")
@@ -192,6 +194,7 @@
                     total[at, :] = spectrum
                     return carry
                 if outer == 0:
+                    spectrum = spectrum * gain
                     data_term[at, :] = data_term[at, :] * spectrum
                 a_high, a_low = split(data_term[at, :] + prior_gain[at, :] * spectrum)
                 m_high[at, :], m_low[at, :] = split(dot3(a_high, a_low, zh_ref[...], zl_ref[...]))
@@ -214,64 +217,77 @@
         each_peer(lambda peer: back_copy(c, peer, me).start())
         target[me, c] = back[c, me]
 
-    def denoise(outer, index, low, high):
+    def denoise(outer, index, spans):
         dual_x, dual_y, dual_z = duals[3 * index : 3 * index + 3]
-        wide = (high - low + 2) * GROUP
-        column = lax.broadcasted_iota(jnp.int32, (wide, nz), 1)
-        not_first = jnp.where(column > 0, 1.0, 0.0)
-        not_last = jnp.where(column < nz - 1, 1.0, 0.0)
-        edge = low == 0 or high == groups
+        members = [(g, low <= g < high) for low, high in spans for g in range(low - 1, high + 1)]
+        wide = len(members) * GROUP
+        lane = lax.broadcasted_iota(jnp.int32, (wide, LANES), 1)
+        is_first, is_last = lane == 0, lane == LANES - 1
+        nothing = jnp.zeros((wide, LANES), f32)
+        edge = members[0][0] < 0
         if edge:
-            line = lax.broadcasted_iota(jnp.int32, (wide, nz), 0) + (me * rows + (low - 1) * GROUP)
-            inside = jnp.where((line >= 0) & (line < nx), 1.0, 0.0)
-
-        def bend_x(value):
-            return pltpu.roll(value, 1, 0) + pltpu.roll(value, wide - 1, 0) - 2.0 * value
-
-        def bend_z(value):
-            return (
-                pltpu.roll(value, 1, 1) * not_first
-                + pltpu.roll(value, nz - 1, 1) * not_last
-                - 2.0 * value
+            place = lax.broadcasted_iota(jnp.int32, (GROUP, nz), 0) * 0 + me
+            inside = jnp.concatenate(
+                [
+                    jnp.where(place > 0, 1.0, 0.0)
+                    if g < 0
+                    else jnp.where(place < n - 1, 1.0, 0.0)
+                    if g >= groups
+                    else jnp.ones((GROUP, nz), f32)
+                    for g, _ in members
+                ],
+                axis=0,
             )
 
-        def neighbours(get, y):
-            below = get(jnp.maximum(y - 1, 0)) * jnp.where(y > 0, 1.0, 0.0)
-            above = get(jnp.minimum(y + 1, ny - 1)) * jnp.where(y < ny - 1, 1.0, 0.0)
-            return below + above - 2.0 * get(y)
-
-        def goal(y):
+        def sum_x(value):
+            return pltpu.roll(value, 1, 0) + pltpu.roll(value, wide - 1, 0)
+
+        def sum_z(value):
+            pieces = [value[:, z : z + LANES] for z in range(0, nz, LANES)]
+            ups = [nothing] + [pltpu.roll(piece, 1, 1) for piece in pieces]
+            downs = [pltpu.roll(piece, LANES - 1, 1) for piece in pieces] + [nothing]
+            return jnp.concatenate(
+                [
+                    jnp.where(is_first, ups[z], ups[z + 1])
+                    + jnp.where(is_last, downs[z + 1], downs[z])
+                    for z in range(len(pieces))
+                ],
+                axis=1,
+            )
+
+        def collect(y, carry):
             pieces = []
-            for g in range(low - 1, high + 1):
+            for g, _ in members:
                 if g < 0:
                     pieces.append(halo[0, y])
                 elif g >= groups:
                     pieces.append(halo[1, y])
                 else:
                     pieces.append(target[y, seat[g][0], seat[g][1]])
-            return jnp.concatenate(pieces, axis=0)
-
-        def reader(ref):
-            return lambda y: ref[y, 0:wide, :]
-
-        scale = 1.0 / (1.0 + step_dual * huber_eps / bound_dual)
+            goal[y + 1, 0:wide, :] = jnp.concatenate(pieces, axis=0)
+            return carry
+
+        lax.fori_loop(0, ny, collect, 0)
         for sweep in range(PASSES):
-            origin = goal if sweep == 0 else reader(lead)
-            base = goal if sweep == 0 else reader(field)
+            origin = goal if sweep == 0 else lead
             fresh = outer == 0 and sweep == 0
 
             def rise(y):
-                here = origin(y)
-                bends = (bend_x(here), neighbours(origin, y), bend_z(here))
-                if fresh:
-                    raised = [bend * (step_dual * scale) for bend in bends]
-                else:
+                here = origin[y, 0:wide, :]
+                twice = here + here
+                raised = [
+                    sum_x(here) - twice,
+                    origin[y - 1, 0:wide, :] + origin[y + 1, 0:wide, :] - twice,
+                    sum_z(here) - twice,
+                ]
+                if not fresh:
                     raised = [
-                        dual[y] * scale + bend * (step_dual * scale)
-                        for dual, bend in zip((dual_x, dual_y, dual_z), bends)
+                        dual[y] + bend for dual, bend in zip((dual_x, dual_y, dual_z), raised)
                     ]
                 norm = raised[0] * raised[0] + raised[1] * raised[1] + raised[2] * raised[2]
-                shrink = lax.rsqrt(jnp.maximum(1.0, norm * (1.0 / bound_dual**2)))
+                shrink = lax.rsqrt(
+                    jnp.maximum(1.0 / relax**2, norm * (1.0 / (bound_dual * relax) ** 2))
+                )
                 if edge:
                     shrink = shrink * inside
                 dual_x[y] = raised[0] * shrink
@@ -279,34 +295,44 @@
                 dual_z[y] = raised[2] * shrink
 
             def fall(y):
+                in_x, in_y, in_z = dual_x[y], dual_y[y], dual_z[y]
+                middle = in_x + in_y + in_z
                 adjoint = (
-                    bend_x(dual_x[y]) + neighbours(lambda at: dual_y[at], y) + bend_z(dual_z[y])
-                )
-                old = base(y)
-                updated = (old - step_primal * adjoint + step_primal * goal(y)) * (
-                    1.0 / (1.0 + step_primal)
-                )
+                    sum_x(in_x) + (dual_y[y - 1] + dual_y[y + 1]) + sum_z(in_z) - (middle + middle)
+                ) * (step_primal * step_dual / (1.0 + step_primal))
+                if sweep == 0:
+                    old = goal[y, 0:wide, :]
+                    updated = old - adjoint
+                else:
+                    old = field[y, 0:wide, :]
+                    updated = (
+                        old * (1.0 / (1.0 + step_primal))
+                        + goal[y, 0:wide, :] * (step_primal / (1.0 + step_primal))
+                        - adjoint
+                    )
                 if sweep < PASSES - 1:
                     if edge:
                         updated = updated * inside
-                    lead[y, 0:wide, :] = 2.0 * updated - old
+                    lead[y, 0:wide, :] = updated + updated - old
                     field[y, 0:wide, :] = updated
-                elif outer < OUTER - 1:
-                    for g in range(low, high):
-                        start = (g - low + 1) * GROUP
-                        current[y, seat[g][0], seat[g][1]] = updated[start : start + GROUP, :]
-                else:
-                    out_ref[y, low * GROUP : high * GROUP, :] = updated[GROUP : wide - GROUP, :]
-
-            rise(0)
+                    return
+                for i, (g, own) in enumerate(members):
+                    if own:
+                        lines = updated[i * GROUP : (i + 1) * GROUP, :]
+                        if outer < OUTER - 1:
+                            current[y - 1, seat[g][0], seat[g][1]] = lines
+                        else:
+                            out_ref[y - 1, g * GROUP : (g + 1) * GROUP, :] = lines * (1.0 / gain)
+
+            rise(1)
 
             def body(y, carry):
                 rise(y)
                 fall(y - 1)
                 return carry
 
-            lax.fori_loop(1, ny, body, 0)
-            fall(ny - 1)
+            lax.fori_loop(2, ny + 1, body, 0)
+            fall(ny)
 
     lax.fori_loop(0, ny, stage, 0)
     pl.semaphore_wait(barrier, n - 1)
@@ -321,6 +347,9 @@
     def _():
         halo[1] = jnp.zeros(halo.shape[1:], f32)
 
+    for ref in [goal, lead] + list(duals[1::3]):
+        ref[0] = jnp.zeros(ref.shape[1:], f32)
+        ref[ny + 1] = jnp.zeros(ref.shape[1:], f32)
     make_tables()
     make_filter()
     quarter = groups // 4
@@ -358,16 +387,15 @@
 
         done = 0
         if chunks > 1:
-            denoise(outer, 0, 0, quarter)
-            denoise(outer, 1, groups - quarter, groups)
+            denoise(outer, 0, [(0, quarter), (groups - quarter, groups)])
             done = quarter
             if outer < OUTER - 1:
                 for c in range(done):
                     send_forward(c)
             arrive(range(quarter + 1, chunks))
-            denoise(outer, 2, quarter, groups - quarter)
+            denoise(outer, 1, [(quarter, groups - quarter)])
         else:
-            denoise(outer, 0, 0, groups)
+            denoise(outer, 0, [(0, groups)])
 
         @pl.when(me < n - 1)
         def _():
@@ -419,10 +447,10 @@
     groups = rows // GROUP
     if groups % 4 == 0:
         order = [(c, groups - 1 - c) for c in range(groups // 2)]
-        sizes = [groups // 4, groups // 4, groups // 2]
+        sizes = [groups // 2 + 4, groups // 2 + 2]
     else:
         order = [tuple(range(groups))]
-        sizes = [groups]
+        sizes = [groups + 2]
     chunks, slots = len(order), len(order[0])
     lines, columns = tilt_index.shape
     depth, width = -(-lines // 128) * 128, -(-columns // 128) * 128
@@ -431,8 +459,8 @@
     tiles = tiles.transpose(0, 1, 3, 2, 4).reshape(-1, LANES)
     vmem = pl.BlockSpec(memory_space=pltpu.VMEM)
     smem = pl.BlockSpec(memory_space=pltpu.SMEM)
-    tile_rows = [(size + 2) * GROUP for size in sizes]
-    scratch_tile = pltpu.VMEM((ny, max(tile_rows), nz), f32)
+    tile_rows = [size * GROUP for size in sizes]
+    scratch_tile = pltpu.VMEM((ny + 2, max(tile_rows), nz), f32)
     plane = pltpu.VMEM((nx, nz), f32)
     blocks = pltpu.VMEM((chunks, n, slots, GROUP, nz), f32)
     cells = pltpu.VMEM((ny, chunks, slots, GROUP, nz), f32)
@@ -456,7 +484,8 @@
             pltpu.VMEM((2, ny, GROUP, nz), f32),
             scratch_tile,
             scratch_tile,
-            [pltpu.VMEM((ny, size, nz), f32) for size in tile_rows for _ in range(3)],
+            scratch_tile,
+            [pltpu.VMEM((ny + 2, size, nz), f32) for size in tile_rows for _ in range(3)],
             cells,
             pltpu.VMEM((width, depth), f32),
             semaphores,

time: 149 us -> 138 us (0.926)
  Pallas kernels: 146 us -> 135 us
    pallas_call x1, Pallas kernels: 146 us -> 135 us  [local(): pl.pallas_call(functools.partial(kernel, n, rows, order), out_shape=jax.S...]
where the time goes in v3:
time: 138 us
  Pallas kernels  135 us (98%)
  local copies, waits for them, and re-layouts  2.81 us (2%)
    pallas_call x1, Pallas kernels, local(): pl.pallas_call(functools.partial(kernel, n, rows, order), out_shape=jax.S...  135 us
    transpose x1, local copies, waits for them, and re-layouts, local(): return jnp.swapaxes(result, 0, 1)  2.81 us

profile of v3, /device:TPU:16, one launch (start us, length us, event | category | flops | bytes accessed | tf_op | source)
XLA Modules:
  0.0 138.0 jit_solution(10861793941421056784)
XLA Ops:
  0.0 135.2 %shard_map.100 = f32[16,64,256]{2,1,0:T(8,128)} custom-call(f32[2048,128]{1,0:T(8,128)} %bitcast.9, f32[16]{0:T(128)} %table_ref.1, s32[129,513]{1,0:T(8,128)} %bitcast.10, s32[129,513]{1,0:T(8,128)} %bitcast.11, f32[128,1024]{1,0:T(8,128)} %constant.12.clone.cos_ref, f32[128,1024]{1,0:T(8,128)} %constant.13.clone.sin_ref, ...), custom_call_target="tpu_custom_call" | custom-call | tf_op jit(solution)/shard_map/pallas_call | solution.py:468
  135.2 2.8 %copy.11 = f32[64,16,256]{2,1,0:T(8,128)} copy(f32[64,16,256]{2,0,1:T(8,128)} %bitcast.8) | data formatting | bytes 2097152 | tf_op jit(solution)/shard_map/transpose | solution.py:502

commit v4 on v3

--- a/solution.py
+++ b/solution.py
@@ -13,6 +13,7 @@
 PASSES = 2
 GROUP = 8
 LANES = 128
+STEP = 2
 
 step_dual = 0.14
 step_primal = 0.14
@@ -221,9 +222,8 @@
         dual_x, dual_y, dual_z = duals[3 * index : 3 * index + 3]
         members = [(g, low <= g < high) for low, high in spans for g in range(low - 1, high + 1)]
         wide = len(members) * GROUP
-        lane = lax.broadcasted_iota(jnp.int32, (wide, LANES), 1)
-        is_first, is_last = lane == 0, lane == LANES - 1
-        nothing = jnp.zeros((wide, LANES), f32)
+        step = STEP * GROUP
+        strips = [(r, min(r + step, wide)) for r in range(0, wide, step)]
         edge = members[0][0] < 0
         if edge:
             place = lax.broadcasted_iota(jnp.int32, (GROUP, nz), 0) * 0 + me
@@ -239,21 +239,30 @@
                 axis=0,
             )
 
-        def sum_x(value):
-            return pltpu.roll(value, 1, 0) + pltpu.roll(value, wide - 1, 0)
+        def sum_x(ref, y, start, stop):
+            first, last = max(start - GROUP, 0), min(stop + GROUP, wide)
+            value = ref[y, first:last, :]
+            both = pltpu.roll(value, 1, 0) + pltpu.roll(value, last - first - 1, 0)
+            return both[start - first : stop - first, :]
 
         def sum_z(value):
             pieces = [value[:, z : z + LANES] for z in range(0, nz, LANES)]
+            nothing = jnp.zeros_like(pieces[0])
+            lane = lax.broadcasted_iota(jnp.int32, pieces[0].shape, 1)
             ups = [nothing] + [pltpu.roll(piece, 1, 1) for piece in pieces]
             downs = [pltpu.roll(piece, LANES - 1, 1) for piece in pieces] + [nothing]
             return jnp.concatenate(
                 [
-                    jnp.where(is_first, ups[z], ups[z + 1])
-                    + jnp.where(is_last, downs[z + 1], downs[z])
+                    jnp.where(lane == 0, ups[z], ups[z + 1])
+                    + jnp.where(lane == LANES - 1, downs[z + 1], downs[z])
                     for z in range(len(pieces))
                 ],
                 axis=1,
             )
+
+        def at_edge(start, stop):
+            some = [g for g, _ in members[start // GROUP : stop // GROUP]]
+            return min(some) < 0 or max(some) >= groups
 
         def collect(y, carry):
             pieces = []
@@ -273,56 +282,64 @@
             fresh = outer == 0 and sweep == 0
 
             def rise(y):
-                here = origin[y, 0:wide, :]
-                twice = here + here
-                raised = [
-                    sum_x(here) - twice,
-                    origin[y - 1, 0:wide, :] + origin[y + 1, 0:wide, :] - twice,
-                    sum_z(here) - twice,
-                ]
-                if not fresh:
+                for start, stop in strips:
+                    here = origin[y, start:stop, :]
+                    twice = here + here
                     raised = [
-                        dual[y] + bend for dual, bend in zip((dual_x, dual_y, dual_z), raised)
+                        sum_x(origin, y, start, stop) - twice,
+                        origin[y - 1, start:stop, :] + origin[y + 1, start:stop, :] - twice,
+                        sum_z(here) - twice,
                     ]
-                norm = raised[0] * raised[0] + raised[1] * raised[1] + raised[2] * raised[2]
-                shrink = lax.rsqrt(
-                    jnp.maximum(1.0 / relax**2, norm * (1.0 / (bound_dual * relax) ** 2))
-                )
-                if edge:
-                    shrink = shrink * inside
-                dual_x[y] = raised[0] * shrink
-                dual_y[y] = raised[1] * shrink
-                dual_z[y] = raised[2] * shrink
+                    if not fresh:
+                        raised = [
+                            dual[y, start:stop, :] + bend
+                            for dual, bend in zip((dual_x, dual_y, dual_z), raised)
+                        ]
+                    norm = raised[0] * raised[0] + raised[1] * raised[1] + raised[2] * raised[2]
+                    shrink = lax.rsqrt(
+                        jnp.maximum(1.0 / relax**2, norm * (1.0 / (bound_dual * relax) ** 2))
+                    )
+                    if at_edge(start, stop):
+                        shrink = shrink * inside[start:stop, :]
+                    dual_x[y, start:stop, :] = raised[0] * shrink
+                    dual_y[y, start:stop, :] = raised[1] * shrink
+                    dual_z[y, start:stop, :] = raised[2] * shrink
 
             def fall(y):
-                in_x, in_y, in_z = dual_x[y], dual_y[y], dual_z[y]
-                middle = in_x + in_y + in_z
-                adjoint = (
-                    sum_x(in_x) + (dual_y[y - 1] + dual_y[y + 1]) + sum_z(in_z) - (middle + middle)
-                ) * (step_primal * step_dual / (1.0 + step_primal))
-                if sweep == 0:
-                    old = goal[y, 0:wide, :]
-                    updated = old - adjoint
-                else:
-                    old = field[y, 0:wide, :]
-                    updated = (
-                        old * (1.0 / (1.0 + step_primal))
-                        + goal[y, 0:wide, :] * (step_primal / (1.0 + step_primal))
-                        - adjoint
-                    )
-                if sweep < PASSES - 1:
-                    if edge:
-                        updated = updated * inside
-                    lead[y, 0:wide, :] = updated + updated - old
-                    field[y, 0:wide, :] = updated
-                    return
-                for i, (g, own) in enumerate(members):
-                    if own:
-                        lines = updated[i * GROUP : (i + 1) * GROUP, :]
-                        if outer < OUTER - 1:
-                            current[y - 1, seat[g][0], seat[g][1]] = lines
-                        else:
-                            out_ref[y - 1, g * GROUP : (g + 1) * GROUP, :] = lines * (1.0 / gain)
+                for start, stop in strips:
+                    in_x, in_y, in_z = [
+                        dual[y, start:stop, :] for dual in (dual_x, dual_y, dual_z)
+                    ]
+                    middle = in_x + in_y + in_z
+                    adjoint = (
+                        sum_x(dual_x, y, start, stop)
+                        + (dual_y[y - 1, start:stop, :] + dual_y[y + 1, start:stop, :])
+                        + sum_z(in_z)
+                        - (middle + middle)
+                    ) * (step_primal * step_dual / (1.0 + step_primal))
+                    if sweep == 0:
+                        old = goal[y, start:stop, :]
+                        updated = old - adjoint
+                    else:
+                        old = field[y, start:stop, :]
+                        updated = (
+                            old * (1.0 / (1.0 + step_primal))
+                            + goal[y, start:stop, :] * (step_primal / (1.0 + step_primal))
+                            - adjoint
+                        )
+                    if sweep < PASSES - 1:
+                        if at_edge(start, stop):
+                            updated = updated * inside[start:stop, :]
+                        lead[y, start:stop, :] = updated + updated - old
+                        field[y, start:stop, :] = updated
+                        continue
+                    for i, (g, own) in enumerate(members):
+                        if own and start <= i * GROUP < stop:
+                            lines = updated[i * GROUP - start : (i + 1) * GROUP - start, :]
+                            if outer < OUTER - 1:
+                                current[y - 1, seat[g][0], seat[g][1]] = lines
+                            else:
+                                out_ref[y - 1, g * GROUP : (g + 1) * GROUP, :] = lines * (1.0 / gain)
 
             rise(1)
 
@@ -387,13 +404,10 @@
 
         done = 0
         if chunks > 1:
-            denoise(outer, 0, [(0, quarter), (groups - quarter, groups)])
             done = quarter
-            if outer < OUTER - 1:
-                for c in range(done):
-                    send_forward(c)
             arrive(range(quarter + 1, chunks))
-            denoise(outer, 1, [(quarter, groups - quarter)])
+            denoise(outer, 0, [(0, groups)])
+            done = 0
         else:
             denoise(outer, 0, [(0, groups)])
 
@@ -447,7 +461,7 @@
     groups = rows // GROUP
     if groups % 4 == 0:
         order = [(c, groups - 1 - c) for c in range(groups // 2)]
-        sizes = [groups // 2 + 4, groups // 2 + 2]
+        sizes = [groups + 2]
     else:
         order = [tuple(range(groups))]
         sizes = [groups + 2]

time: 138 us -> 137 us (level); the launches traced: 138 us -> 135 us
  Pallas kernels: 135 us -> 132 us
    pallas_call x1, Pallas kernels: 135 us -> 132 us  [local(): pl.pallas_call(functools.partial(kernel, n, rows, order), out_shape=jax.S...]
where the time goes in v4:
time: 137 us; the launch traced here: 135 us
  Pallas kernels  132 us (96%)
  local copies, waits for them, and re-layouts  2.81 us (2%)
    pallas_call x1, Pallas kernels, local(): pl.pallas_call(functools.partial(kernel, n, rows, order), out_shape=jax.S...  132 us
    transpose x1, local copies, waits for them, and re-layouts, local(): return jnp.swapaxes(result, 0, 1)  2.81 us

profile of v4, /device:TPU:16, one launch (start us, length us, event | category | flops | bytes accessed | tf_op | source)
XLA Modules:
  0.0 134.9 jit_solution(18169351738180319720)
XLA Ops:
  0.0 132.1 %shard_map.100 = f32[16,64,256]{2,1,0:T(8,128)} custom-call(f32[2048,128]{1,0:T(8,128)} %bitcast.9, f32[16]{0:T(128)} %table_ref.1, s32[129,513]{1,0:T(8,128)} %bitcast.10, s32[129,513]{1,0:T(8,128)} %bitcast.11, f32[128,1024]{1,0:T(8,128)} %constant.12.clone.cos_ref, f32[128,1024]{1,0:T(8,128)} %constant.13.clone.sin_ref, ...), custom_call_target="tpu_custom_call" | custom-call | tf_op jit(solution)/shard_map/pallas_call | solution.py:482
  132.1 2.8 %copy.11 = f32[64,16,256]{2,1,0:T(8,128)} copy(f32[64,16,256]{2,0,1:T(8,128)} %bitcast.8) | data formatting | bytes 2097152 | tf_op jit(solution)/shard_map/transpose | solution.py:516
